TPU v7x, 32 devices: a whole 2x2x4 slice. The times are simulated.
32 devices in a mesh: wide: 8 (over y, x, core), narrow: 4 (over z).
Axes of the slice: x: 2, y: 2, z: 4, core: 2. Of those that a mesh axis runs over, the one named last changes fastest.
Arguments:
- batch_index: int32 [256], P('narrow'), may hold values from 0 to 255
- train_features: float32 [1024, 1024], P('narrow'), may hold values from -6 to 6
- train_labels: float32 [1024, 1000], P('narrow'), may hold values from -12 to 12
- centers: float32 [8192, 1024], P(('wide', 'narrow')), may hold values from -6 to 6
- weights: float32 [8192, 1000], P(('wide', 'narrow')), may hold values from -6 to 6
Outputs:
- new_weights: float32 [8192, 1000], P(('wide', 'narrow'))
- residual: float32 [256, 1000], P('narrow')
Inputs may be any that keep to these rules, and one draw needn't show every extreme that they name: `batch_index`: entry i names a row of the training shard held by narrow index i // 64.
All inputs are finite; a program needn't handle non-finite values.
Results may differ from a plain program's by a relative error of at most 0.0001.
Values sent between devices are 32-bit elements; how exact they have to be, the bound alone decides.
A program may use at most 64 MiB of HBM per device.

v0:
```python
import math

import jax
import jax.numpy as jnp
from jax import lax
from jax.sharding import PartitionSpec as P

step_size = 1.0


def per_device(batch_index, train_features, train_labels, centers, weights):
    rows = jnp.take(train_features, batch_index, axis=0)
    targets = jnp.take(train_labels, batch_index, axis=0)
    features = centers.shape[1]
    center_sq = jnp.sum(centers * centers, axis=1)
    count = centers.shape[0] * lax.axis_size("wide") * lax.axis_size("narrow")
    scale = 1.0 / math.sqrt(count)
    piece = lax.all_gather(rows, "narrow", axis=0, tiled=True)
    inner = jnp.dot(
        piece, centers.T, precision=lax.Precision.HIGHEST, preferred_element_type=jnp.float32
    )
    piece_sq = jnp.sum(piece * piece, axis=1)
    kernel = jnp.exp(
        (2.0 * features - piece_sq[:, None] - center_sq[None, :] + 2.0 * inner) / 128.0
    )
    batch = kernel.shape[0]
    kern_rows = kernel
    local = lax.psum_scatter(
        jnp.dot(
            kern_rows, weights, precision=lax.Precision.HIGHEST, preferred_element_type=jnp.float32
        ),
        "narrow",
        scatter_dimension=0,
        tiled=True,
    )
    predicted = lax.psum(local, "wide") * scale
    residual = predicted - targets
    kern_rows = kernel
    delta = lax.dot_general(
        kern_rows,
        lax.all_gather(residual, "narrow", axis=0, tiled=True),
        (((0,), (0,)), ((), ())),
        precision=lax.Precision.HIGHEST,
        preferred_element_type=jnp.float32,
    )
    new_weights = weights - step_size / batch * delta
    return (new_weights, residual)


def solution(mesh):
    in_specs = (
        P("narrow"),
        P("narrow", None),
        P("narrow", None),
        P(("wide", "narrow"), None),
        P(("wide", "narrow"), None),
    )
    out_specs = (P(("wide", "narrow"), None), P("narrow", None))
    return jax.shard_map(
        per_device, mesh=mesh, in_specs=in_specs, out_specs=out_specs, check_vma=False
    )
```

profile of v0, /device:TPU:0, one launch (start us, length us, event | category | flops | bytes accessed | tf_op | source)
XLA Modules:
  0.0 160.9 jit_solution(7561517133553205740)
XLA Ops:
  7.2 0.0 copy-start
  7.2 0.0 copy-start.5
  7.2 0.0 all-gather.2.cloned.1.call-start
  7.2 0.7 compare_and_fusion
  8.0 0.0 copy-done.5
  8.0 0.4 copy-done
  8.4 0.0 copy-start.1
  8.4 0.7 gather_fusion
  9.1 0.8 broadcast_select_fusion
  9.9 0.0 all-gather.2.cloned.1.call-update
  9.9 0.0 reduce-scatter.2.cloned.1.call-start
  10.0 0.0 copy-done.1
  10.0 0.1 multiply_reduce_fusion
  10.1 30.7 %all-gather.2.cloned.1.call-done = f32[256,1024]{1,0:T(8,128)} async-done(((f32[64,1024]{1,0:T(8,128)}), f32[256,1024]{1,0:T(8,128)}) %all-gather.2.cloned.1.call-update) | async-done | bytes 1048592 | tf_op jit(solution)/shard_map/all_gather | solution.py:18
  40.9 0.0 copy-start.2
  40.9 1.5 multiply_reduce_fusion.1
  42.4 0.1 copy-done.2
  42.4 0.0 copy-start.3
  42.4 1.1 fusion.3
  43.5 0.1 copy-done.3
  43.6 2.0 %fusion.4 = f32[256,1000]{1,0:T(8,128)} fusion(f32[256,256]{1,0:T(8,128)S(1)} %fusion.3, f32[256,1000]{0,1:T(8,128)S(1)} %copy-done.3), kind=kOutput, calls=%fused_computation.16 | convolution fusion | flops 786432000 | bytes 2310144 | tf_op jit(solution)/shard_map/dot_general | solution.py:29
  45.7 0.0 reduce-scatter.2.cloned.1.call-update
  45.7 0.0 all-reduce.2.cloned.1.call-start
  45.7 26.8 %reduce-scatter.2.cloned.1.call-done = f32[64,1000]{1,0:T(8,128)} async-done(((f32[256,1000]{1,0:T(8,128)}), f32[64,1000]{1,0:T(8,128)}) %reduce-scatter.2.cloned.1.call-update) | async-done | bytes 256016 | tf_op jit(solution)/shard_map/reduce_scatter | solution.py:28
  72.5 0.0 all-reduce.2.cloned.1.call-update
  72.5 1.5 copy.7
  74.1 1.4 gather_fusion.1
  75.5 52.5 %all-reduce.2.cloned.1.call-done = f32[64,1000]{1,0:T(8,128)} async-done(((f32[64,1000]{1,0:T(8,128)}), f32[64,1000]{1,0:T(8,128)}) %all-reduce.2.cloned.1.call-update) | async-done | bytes 256016 | tf_op jit(solution)/shard_map/psum | solution.py:36
  128.0 1.1 select_subtract_fusion
  129.1 0.0 copy-start.4
  129.1 22.5 %all_gather.7 = f32[256,1000]{1,0:T(8,128)S(1)} all-gather(f32[64,1000]{1,0:T(8,128)S(1)} %select_subtract_fusion), channel_id=1, replica_groups=mesh['wide'=8,'narrow'=4] {'narrow'}, dimensions={0}, use_global_device_ids=true | all-gather | bytes 1280000 | tf_op jit(solution)/shard_map/all_gather | solution.py:41
  151.6 0.0 copy-done.4
  151.6 2.8 %fusion = f32[256,1000]{0,1:T(8,128)} fusion(f32[256,1000]{0,1:T(8,128)S(1)} %copy-done.3, f32[256,256]{1,0:T(8,128)S(1)} %fusion.3, f32[256,1000]{1,0:T(8,128)S(1)} %all_gather.7), kind=kOutput, calls=%fused_computation.3 | convolution fusion | flops 786944000 | bytes 3334144 | tf_op jit(solution)/shard_map/dot_general | solution.py:39
  (3 shorter events, 0.0 us)
Async XLA Ops:
  7.2 1.3 copy-start
  7.2 0.8 copy-start.5
  7.2 33.7 %all-gather.2.cloned.1.call-start = ((), (), s32[]{:S(2)}) async-start(), calls=%async_computation.1 | async-start | bytes 1310720 | tf_op jit(solution)/shard_map/all_gather | solution.py:18
  8.4 1.6 copy-start.1
  9.9 62.6 %reduce-scatter.2.cloned.1.call-start = ((), (), s32[]{:S(2)}) async-start(), calls=%async_computation.2 | async-start | bytes 1310720 | tf_op jit(solution)/shard_map/reduce_scatter | solution.py:28
  40.9 1.5 copy-start.2
  42.4 1.2 copy-start.3
  45.7 82.3 %all-reduce.2.cloned.1.call-start = ((), (), s32[]{:S(2)}) async-start(), calls=%async_computation.3 | async-start | bytes 524288 | tf_op jit(solution)/shard_map/psum | solution.py:36
  129.1 22.5 %copy-start.4 = (f32[64,1000]{1,0:T(8,128)}, f32[64,1000]{1,0:T(8,128)S(1)}, u32[]{:S(2)}) copy-start(f32[64,1000]{1,0:T(8,128)S(1)} %select_subtract_fusion) | copy-start | bytes 768004
Sparse Core Ops, SparseCore 0:
  10.1 30.6 all-gather.1
  45.8 26.6 reduce-scatter.1
  75.6 52.3 all-reduce.1
where the time goes:
time: 161 us
  waiting for transfers between devices  110 us (68%)
  blocking collectives  22.5 us (14%)
  between operations  13.8 us (9%)
  matrix products  5.91 us (4%)
  other arithmetic  4.28 us (3%)
  local copies, waits for them, and re-layouts  4.26 us (3%)
    psum x1, waiting for transfers between devices, per_device(): predicted = lax.psum(local, 'wide') * scale  52.5 us
    all_gather x1, waiting for transfers between devices, per_device(): piece = lax.all_gather(rows, 'narrow', axis=0, tiled=True)  30.7 us
    reduce_scatter x1, waiting for transfers between devices, per_device(): lax.psum_scatter(jnp.dot(kern_rows, weights, precision=lax.Precision.HIGH...  26.8 us
    all_gather x1, blocking collectives, per_device(): lax.all_gather(residual, 'narrow', axis=0, tiled=True)  22.5 us
  transfers between devices with their start and end apart: 3, of which 3 were waited for; matrix products, arithmetic and copies ran while one was open for 2% of the time, Pallas kernels for 0%

commit v1 on v0

v1 whole, which is shorter than its diff:
```python
import functools
import math

import jax
import jax.numpy as jnp
from jax import lax
from jax.experimental import pallas as pl
from jax.experimental.pallas import tpu as pltpu
from jax.sharding import PartitionSpec as P

step_size = 1.0
MESH = pl.DeviceIdType.MESH
HIGHEST = lax.Precision.HIGHEST
SUB = 8


def dot(a, b, dims):
    return lax.dot_general(
        a, b, (dims, ((), ())), precision=HIGHEST, preferred_element_type=jnp.float32
    )


def plan(wide, block):
    stages, rows = [], block
    for _ in range(wide.bit_length() - 1):
        halves = rows >= 2 * SUB
        rows = rows // 2 if halves else rows
        stages.append((rows, halves))
    return stages


def step_kernel(
    wide, narrow, count, index_ref, tf_hbm, lab_hbm, cen_hbm, wgt_hbm, out_hbm, res_hbm,
    tf, lab, cen, wgt, rows, kern, part, resid, tgt, got, zgot, load_sem,
    zrow_s, zrow_r, crow_s, crow_r, red_s, red_r, zred_s, zred_r, zag_s, zag_r, ag_s, ag_r, out_sem,
):
    w, n = lax.axis_index("wide"), lax.axis_index("narrow")
    block = index_ref.shape[0]
    batch = block * narrow
    features = cen.shape[1]
    stages = plan(wide, block)
    nst = len(stages)
    core = w % 2
    partner = (w + 1 - 2 * core, n)
    up = [2**k for k in range(1, nst)]
    masks = [1] + [jnp.where(core == 0, p, q) for p, q in zip(up, up[::-1])]
    side = [core] + [(w // m) % 2 for m in masks[1:]]
    peer = [partner] + [(w + m * (1 - 2 * s), n) for m, s in zip(masks[1:], side[1:])]
    start = [0]
    for s, (held, halves) in zip(side, stages):
        start.append(start[-1] + (s * held if halves else 0))
    start = [0] + [pl.multiple_of(s, SUB) for s in start[1:]]
    half = stages[0][0]

    loads = [
        pltpu.make_async_copy(src, dst, load_sem.at[i])
        for i, (src, dst) in enumerate(((tf_hbm, tf), (cen_hbm, cen), (wgt_hbm, wgt), (lab_hbm, lab)))
    ]
    for load in loads:
        load.start()
    zpeers = [(w, lax.rem(n + k, narrow)) for k in range(1, narrow)]
    barrier = pltpu.get_barrier_semaphore()
    for p in zpeers + peer:
        pl.semaphore_signal(barrier, inc=1, device_id=p, device_id_type=MESH)

    def copy(src, dst, ssem, rsem, to):
        return pltpu.make_async_remote_copy(
            src_ref=src, dst_ref=dst, send_sem=ssem, recv_sem=rsem, device_id=to, device_id_type=MESH
        )

    sent = []

    def send(*args, later=True):
        c = copy(*args)
        c.start()
        if later:
            sent.append(c)
        return c

    loads[0].wait()
    for g in range(block // SUB):
        picked = [tf[pl.ds(index_ref[g * SUB + i], 1), :] for i in range(SUB)]
        rows[n, pl.ds(g * SUB, SUB), :] = jnp.concatenate(picked, axis=0)
    pl.semaphore_wait(barrier, len(zpeers) + nst)

    mine = pl.ds(start[1], half)
    other = pl.ds(pl.multiple_of((1 - core) * half, SUB), half)
    for k in range(1, narrow):
        to = (w, lax.rem(n + narrow - k, narrow))
        send(rows.at[n, mine], rows.at[n, mine], zrow_s.at[k], zrow_r.at[k], to)

    loads[1].wait()
    centers = cen[...]
    ones = jnp.ones((SUB, features), jnp.float32)
    center_sq = dot(ones, centers * centers, ((1,), (1,)))[0:1, :]

    def at(k):
        return lax.rem(n + k, narrow)

    def forward(k):
        m = at(k)
        copy(rows.at[m, mine], rows.at[m, mine], zrow_s.at[k], zrow_r.at[k], partner).wait_recv()
        send(rows.at[m, mine], rows.at[m, mine], crow_s.at[k], crow_r.at[k], partner)

    def reduce_copy(j, k):
        m = at(k)
        held, halves = stages[j]
        first = pl.multiple_of(start[j] + (1 - side[j]) * held, SUB) if halves else start[j + 1]
        return (
            part.at[m, pl.ds(first, held)], got[j].at[k], red_s.at[j, k], red_r.at[j, k], peer[j]
        )

    sends = {}

    def begin(k):
        m = at(k)
        if k > 0:
            copy(rows.at[m, other], rows.at[m, other], crow_s.at[k], crow_r.at[k], partner).wait_recv()
        piece = rows[m]
        inner = dot(piece, cen[...], ((1,), (1,)))
        piece_sq = jnp.sum(piece * piece, axis=1, keepdims=True)
        value = jnp.exp((2.0 * features - piece_sq - center_sq + 2.0 * inner) / 128.0)
        kern[m] = value
        if k == 0:
            loads[2].wait()
        part[m] = dot(value, wgt[...], ((1,), (1,)))
        sends[0, k] = send(*reduce_copy(0, k), later=stages[0][1])

    def reduce(j, k):
        m = at(k)
        held, halves = stages[j]
        copy(*reduce_copy(j, k)).wait_recv()
        if not halves:
            sends[j, k].wait_send()
        keep = pl.ds(start[j + 1], held)
        part[m, keep, :] = part[m, keep, :] + got[j][k]
        if j + 1 < nst:
            sends[j + 1, k] = send(*reduce_copy(j + 1, k), later=stages[j + 1][1])
        elif k > 0:
            send(part.at[m, keep], zgot.at[k], zred_s.at[k], zred_r.at[k], (w, m))

    for t in range(narrow + nst):
        if t < narrow:
            begin(t)
        if t + 1 < narrow:
            forward(t + 1)
        for j in range(nst):
            if 0 <= t - 1 - j < narrow:
                reduce(j, t - 1 - j)

    last = stages[-1][0]
    keep = pl.ds(start[nst], last)
    loads[3].wait()
    column = lax.broadcasted_iota(jnp.int32, (1, lab.shape[1]), 1)
    chosen = [jnp.where(column == index_ref[start[nst] + i], 1.0, 0.0) for i in range(last)]
    tgt[...] = dot(jnp.concatenate(chosen, axis=0), lab[...], ((1,), (1,)))
    total = part[n, keep, :]
    for k in range(1, narrow):
        copy(part.at[n, keep], zgot.at[k], zred_s.at[k], zred_r.at[k], partner).wait_recv()
        total = total + zgot[k]
    resid[n, keep, :] = total * (1.0 / math.sqrt(count)) - tgt[...]

    for k in range(1, narrow):
        to = (w, lax.rem(n + narrow - k, narrow))
        send(resid.at[n, keep], resid.at[n, keep], zag_s.at[k], zag_r.at[k], to)

    back = [j for j in range(nst) if stages[j][1]][::-1]

    def spread(i, k):
        m = at(k)
        if i == 0:
            if k > 0:
                copy(resid.at[m, keep], resid.at[m, keep], zag_s.at[k], zag_r.at[k], partner).wait_recv()
        else:
            j = back[i - 1]
            held = stages[j][0]
            sibling = pl.ds(pl.multiple_of(start[j] + (1 - side[j]) * held, SUB), held)
            copy(
                resid.at[m, sibling], resid.at[m, sibling], ag_s.at[j, k], ag_r.at[j, k], peer[j]
            ).wait_recv()
        if i < len(back):
            j = back[i]
            own = pl.ds(start[j + 1], stages[j][0])
            send(resid.at[m, own], resid.at[m, own], ag_s.at[j, k], ag_r.at[j, k], peer[j])

    res_copy = pltpu.make_async_copy(resid.at[n], res_hbm, out_sem.at[0])
    for t in range(narrow + len(back)):
        for i in range(len(back) + 1):
            if 0 <= t - i < narrow:
                spread(i, t - i)
                if i == len(back) and t - i == 0:
                    res_copy.start()

    every = resid[...].reshape(batch, resid.shape[2])
    delta = dot(every, kern[...].reshape(batch, cen.shape[0]), ((0,), (0,)))
    wgt[...] = wgt[...] - step_size / batch * delta
    out_copy = pltpu.make_async_copy(wgt, out_hbm, out_sem.at[1])
    out_copy.start()
    for c in sent:
        c.wait_send()
    res_copy.wait()
    out_copy.wait()


def per_device(batch_index, train_features, train_labels, centers, weights):
    wide, narrow = lax.axis_size("wide"), lax.axis_size("narrow")
    block, features = batch_index.shape[0], centers.shape[1]
    outputs, owned = weights.shape[1], centers.shape[0]
    labels_t, weights_t = train_labels.T, weights.T
    stages = plan(wide, block)
    nst, last = len(stages), stages[-1][0]
    f32, dma = jnp.float32, pltpu.SemaphoreType.DMA
    anywhere = pl.BlockSpec(memory_space=pl.ANY)
    new_weights_t, residual = pl.pallas_call(
        functools.partial(step_kernel, wide, narrow, owned * wide * narrow),
        out_shape=(
            jax.ShapeDtypeStruct(weights_t.shape, f32),
            jax.ShapeDtypeStruct((block, outputs), f32),
        ),
        in_specs=[pl.BlockSpec(memory_space=pltpu.SMEM)] + [anywhere] * 4,
        out_specs=(anywhere, anywhere),
        scratch_shapes=[
            pltpu.VMEM(train_features.shape, f32),
            pltpu.VMEM(labels_t.shape, f32),
            pltpu.VMEM(centers.shape, f32),
            pltpu.VMEM(weights_t.shape, f32),
            pltpu.VMEM((narrow, block, features), f32),
            pltpu.VMEM((narrow, block, owned), f32),
            pltpu.VMEM((narrow, block, outputs), f32),
            pltpu.VMEM((narrow, block, outputs), f32),
            pltpu.VMEM((last, outputs), f32),
            [pltpu.VMEM((narrow, held, outputs), f32) for held, _ in stages],
            pltpu.VMEM((narrow, last, outputs), f32),
            dma((4,)),
            dma((narrow,)), dma((narrow,)),
            dma((narrow,)), dma((narrow,)),
            dma((nst, narrow)), dma((nst, narrow)),
            dma((narrow,)), dma((narrow,)),
            dma((narrow,)), dma((narrow,)),
            dma((nst, narrow)), dma((nst, narrow)),
            dma((2,)),
        ],
        compiler_params=pltpu.CompilerParams(
            collective_id=0, has_side_effects=True, vmem_limit_bytes=60 * 2**20
        ),
    )(batch_index, train_features, labels_t, centers, weights_t)
    return new_weights_t.T, residual


def solution(mesh):
    in_specs = (
        P("narrow"),
        P("narrow", None),
        P("narrow", None),
        P(("wide", "narrow"), None),
        P(("wide", "narrow"), None),
    )
    out_specs = (P(("wide", "narrow"), None), P("narrow", None))
    return jax.shard_map(
        per_device, mesh=mesh, in_specs=in_specs, out_specs=out_specs, check_vma=False
    )
```

time: 161 us -> 57.2 us (0.36)
  the two profiles are of different devices: /device:TPU:0 before, /device:TPU:25 now
where the time goes in v1:
time: 57.2 us; the launch traced here: 57.1 us
  Pallas kernels  53.4 us (93%)
  local copies, waits for them, and re-layouts  2.99 us (5%)
  between operations  0.65 us (1%)
    pallas_call x1, Pallas kernels, per_device(): pl.pallas_call(functools.partial(step_kernel, wide, narrow, owned * wide...  53.4 us
    unnamed x4, local copies, waits for them, and re-layouts  2.99 us

profile of v1, /device:TPU:25, one launch (start us, length us, event | category | flops | bytes accessed | tf_op | source)
XLA Modules:
  0.0 57.1 jit_solution(1446205479075911958)
XLA Ops:
  0.6 53.4 %shard_map.68 = (f32[1000,256]{1,0:T(8,128)}, f32[64,1000]{1,0:T(8,128)}) custom-call(s32[64]{0:T(128)} %index_ref.1, f32[256,1024]{1,0:T(8,128)} %tf_hbm.1, f32[1000,256]{1,0:T(8,128)} %bitcast.3, f32[256,1024]{1,0:T(8,128)} %cen_hbm.1, f32[1000,256]{1,0:T(8,128)} %bitcast.4), custom_call_target="tpu_custom_call" | custom-call | tf_op jit(solution)/shard_map/pallas_call | solution.py:214
  54.1 0.0 copy-start
  54.1 2.3 %copy.9 = f32[256,1000]{0,1:T(8,128)} copy(f32[256,1000]{0,1:T(8,128)} %bitcast.5) | data formatting | bytes 2048000
  56.4 0.0 copy-done
  56.4 0.7 %copy.10 = f32[64,1000]{1,0:T(8,128)} copy(f32[64,1000]{1,0:T(8,128)S(1)} %copy-done) | data formatting | bytes 512000
Async XLA Ops:
  54.1 2.3 %copy-start = (f32[64,1000]{1,0:T(8,128)S(1)}, f32[64,1000]{1,0:T(8,128)}, u32[]{:S(2)}) copy-start(f32[64,1000]{1,0:T(8,128)} %get-tuple-element.9) | copy-start | bytes 768004

commit v2 on v1

v2 whole, which is shorter than its diff:
```python
import functools
import math

import jax
import jax.numpy as jnp
from jax import lax
from jax.experimental import pallas as pl
from jax.experimental.pallas import tpu as pltpu
from jax.sharding import PartitionSpec as P

step_size = 1.0
MESH = pl.DeviceIdType.MESH
HIGHEST = lax.Precision.HIGHEST
ROW_DEPTH = 3
SUB = 8


def dot(a, b, dims):
    return lax.dot_general(
        a, b, (dims, ((), ())), precision=HIGHEST, preferred_element_type=jnp.float32
    )


def plan(wide, block):
    stages, rows = [], block
    for _ in range(wide.bit_length() - 1):
        halves = rows >= 2 * SUB
        rows = rows // 2 if halves else rows
        stages.append((rows, halves))
    return stages


def step_kernel(
    wide, narrow, count, index_ref, tf_hbm, lab_hbm, cen_hbm, wgt_hbm, out_hbm, res_hbm,
    tf, lab, cen, wgt, rows, kern, away, part, resid, tgt, got, zgot, load_sem,
    zrow_s, zrow_r, row_s, row_r, pair_s, pair_r, kern_s, kern_r, red_s, red_r, zred_s, zred_r, zag_s, zag_r, ag_s, ag_r, out_sem,
):
    w, n = lax.axis_index("wide"), lax.axis_index("narrow")
    block = index_ref.shape[0]
    batch = block * narrow
    features, owned = cen.shape[2], cen.shape[1]
    stages = plan(wide, block)
    nst = len(stages)
    core = w % 2
    partner = (w + 1 - 2 * core, n)
    up = [2**k for k in range(1, nst)]
    masks = [1] + [jnp.where(core == 0, p, q) for p, q in zip(up, up[::-1])]
    side = [core] + [(w // m) % 2 for m in masks[1:]]
    peer = [partner] + [(w + m * (1 - 2 * s), n) for m, s in zip(masks[1:], side[1:])]
    start = [0]
    for s, (held, halves) in zip(side, stages):
        start.append(start[-1] + (s * held if halves else 0))
    start = [0] + [pl.multiple_of(s, SUB) for s in start[1:]]
    half = stages[0][0]

    loads = [
        pltpu.make_async_copy(src, dst, load_sem.at[i])
        for i, (src, dst) in enumerate(((tf_hbm, tf), (cen_hbm, cen.at[0]), (wgt_hbm, wgt.at[0]), (lab_hbm, lab)))
    ]
    for load in loads:
        load.start()
    zpeers = [(w, lax.rem(n + k, narrow)) for k in range(1, narrow)]
    barrier = pltpu.get_barrier_semaphore()
    for p in zpeers + peer:
        pl.semaphore_signal(barrier, inc=1, device_id=p, device_id_type=MESH)

    def copy(src, dst, ssem, rsem, to):
        return pltpu.make_async_remote_copy(
            src_ref=src, dst_ref=dst, send_sem=ssem, recv_sem=rsem, device_id=to, device_id_type=MESH
        )

    sent = []

    def send(*args, later=True):
        c = copy(*args)
        c.start()
        if later:
            sent.append(c)
        return c

    loads[0].wait()
    for g in range(block // SUB):
        picked = [tf[pl.ds(index_ref[g * SUB + i], 1), :] for i in range(SUB)]
        rows[n, pl.ds(g * SUB, SUB), :] = jnp.concatenate(picked, axis=0)
    pl.semaphore_wait(barrier, len(zpeers) + nst)

    def at(k):
        return lax.rem(n + k, narrow)

    def piece_of(j):
        held = stages[j][0]
        theirs = pl.multiple_of(start[j] + (1 - side[j]) * held, SUB)
        return pl.ds(start[j + 1], held), pl.ds(theirs, held)

    def spread(ref, zsem, sem, back, i, k):
        m = at(k)
        if i == 0:
            if k > 0:
                held = piece_of(back[0])[0]
                copy(ref.at[m, held], ref.at[m, held], zsem[0].at[k], zsem[1].at[k], partner).wait_recv()
        else:
            j = back[i - 1]
            theirs = piece_of(j)[1]
            copy(ref.at[m, theirs], ref.at[m, theirs], sem[0].at[j, k], sem[1].at[j, k], peer[j]).wait_recv()
        if i < len(back) and not (i == len(back) - 1 and back[i] == 0 and ref is rows):
            j = back[i]
            held = piece_of(j)[0]
            send(ref.at[m, held], ref.at[m, held], sem[0].at[j, k], sem[1].at[j, k], peer[j])

    def along_narrow(ref, held, zsem):
        for k in range(1, narrow):
            to = (w, lax.rem(n + narrow - k, narrow))
            send(ref.at[n, held], ref.at[n, held], zsem[0].at[k], zsem[1].at[k], to)

    cuts = [j for j in range(nst) if stages[j][1]][::-1]
    row_cuts = [j for j in cuts if j < ROW_DEPTH]
    mine, other = piece_of(0)
    along_narrow(rows, piece_of(row_cuts[0])[0], (zrow_s, zrow_r))

    loads[1].wait()
    send(cen.at[0], cen.at[1], pair_s.at[0], pair_r.at[0], partner)
    loads[2].wait()
    send(wgt.at[0], wgt.at[1], pair_s.at[1], pair_r.at[1], partner)
    ones = jnp.ones((SUB, features), jnp.float32)

    def squares(o):
        centers = cen[o]
        return dot(ones, centers * centers, ((1,), (1,)))[0:1, :]

    center_sq = [squares(0)]

    def reduce_copy(j, k):
        m = at(k)
        held, halves = stages[j]
        first = start[j] + (1 - side[j]) * held if halves else start[j + 1]
        first = pl.multiple_of(first - core * half, SUB)
        return (
            part.at[m, pl.ds(first, held)], got[j - 1].at[k], red_s.at[j, k], red_r.at[j, k], peer[j]
        )

    sends = {}

    def begin(ks):
        piece = jnp.concatenate([rows[at(k), mine, :] for k in ks], axis=0)
        piece_sq = jnp.sum(piece * piece, axis=1, keepdims=True)
        total = 0.0
        for o in range(2):
            if len(center_sq) == o:
                copy(cen.at[0], cen.at[1], pair_s.at[0], pair_r.at[0], partner).wait_recv()
                center_sq.append(squares(o))
            inner = dot(piece, cen[o], ((1,), (1,)))
            value = jnp.exp((2.0 * features - piece_sq - center_sq[o] + 2.0 * inner) / 128.0)
            for i, k in enumerate(ks):
                this = value[i * half : (i + 1) * half, :]
                if o == 0:
                    kern[at(k), mine, :] = this
                else:
                    away[k] = this
            if o == 1 and 0 in ks:
                copy(wgt.at[0], wgt.at[1], pair_s.at[1], pair_r.at[1], partner).wait_recv()
            total = total + dot(value, wgt[o], ((1,), (1,)))
        for i, k in enumerate(ks):
            part[at(k)] = total[i * half : (i + 1) * half, :]
        for k in ks:
            sends[1, k] = send(*reduce_copy(1, k), later=stages[1][1])
        for k in ks:
            send(away.at[k], kern.at[at(k), mine], kern_s.at[k], kern_r.at[k], partner)

    def reduce(j, k):
        m = at(k)
        held, halves = stages[j]
        copy(*reduce_copy(j, k)).wait_recv()
        if not halves:
            sends[j, k].wait_send()
        keep = pl.ds(pl.multiple_of(start[j + 1] - core * half, SUB), held)
        part[m, keep, :] = part[m, keep, :] + got[j - 1][k]
        if j + 1 < nst:
            sends[j + 1, k] = send(*reduce_copy(j + 1, k), later=stages[j + 1][1])
        elif k > 0:
            send(part.at[m, keep], zgot.at[k], zred_s.at[k], zred_r.at[k], (w, m))

    begin([0])
    for i in range(len(row_cuts)):
        for k in range(1, narrow):
            spread(rows, (zrow_s, zrow_r), (row_s, row_r), row_cuts, i, k)
        if i + 1 < nst:
            reduce(i + 1, 0)
    for i in range(len(row_cuts) + 1, nst):
        reduce(i, 0)
    begin(list(range(1, narrow)))
    for j in range(1, nst):
        for k in range(1, narrow):
            reduce(j, k)

    last = stages[-1][0]
    keep = pl.ds(start[nst], last)
    loads[3].wait()
    column = lax.broadcasted_iota(jnp.int32, (1, lab.shape[1]), 1)
    chosen = [jnp.where(column == index_ref[start[nst] + i], 1.0, 0.0) for i in range(last)]
    tgt[...] = dot(jnp.concatenate(chosen, axis=0), lab[...], ((1,), (1,)))
    own = pl.ds(pl.multiple_of(start[nst] - core * half, SUB), last)
    total = part[n, own, :]
    for k in range(1, narrow):
        copy(part.at[n, own], zgot.at[k], zred_s.at[k], zred_r.at[k], partner).wait_recv()
        total = total + zgot[k]
    resid[n, keep, :] = total * (1.0 / math.sqrt(count)) - tgt[...]

    along_narrow(resid, keep, (zag_s, zag_r))
    res_copy = pltpu.make_async_copy(resid.at[n], res_hbm, out_sem.at[0])
    for t in range(narrow + len(cuts)):
        for i in range(len(cuts) + 1):
            if 0 <= t - i < narrow:
                spread(resid, (zag_s, zag_r), (ag_s, ag_r), cuts, i, t - i)
                if i == len(cuts) and t - i == 0:
                    res_copy.start()

    for k in range(narrow):
        copy(away.at[k], kern.at[at(k), other], kern_s.at[k], kern_r.at[k], partner).wait_recv()
    for c in sent:
        c.wait_send()
    every = resid[...].reshape(batch, resid.shape[2])
    delta = dot(every, kern[...].reshape(batch, owned), ((0,), (0,)))
    wgt[0] = wgt[0] - step_size / batch * delta
    out_copy = pltpu.make_async_copy(wgt.at[0], out_hbm, out_sem.at[1])
    out_copy.start()
    res_copy.wait()
    out_copy.wait()


def per_device(batch_index, train_features, train_labels, centers, weights):
    wide, narrow = lax.axis_size("wide"), lax.axis_size("narrow")
    block, features = batch_index.shape[0], centers.shape[1]
    outputs, owned = weights.shape[1], centers.shape[0]
    labels_t, weights_t = train_labels.T, weights.T
    stages = plan(wide, block)
    nst, last = len(stages), stages[-1][0]
    f32, dma = jnp.float32, pltpu.SemaphoreType.DMA
    anywhere = pl.BlockSpec(memory_space=pl.ANY)
    new_weights_t, residual = pl.pallas_call(
        functools.partial(step_kernel, wide, narrow, owned * wide * narrow),
        out_shape=(
            jax.ShapeDtypeStruct(weights_t.shape, f32),
            jax.ShapeDtypeStruct((block, outputs), f32),
        ),
        in_specs=[pl.BlockSpec(memory_space=pltpu.SMEM)] + [anywhere] * 4,
        out_specs=(anywhere, anywhere),
        scratch_shapes=[
            pltpu.VMEM(train_features.shape, f32),
            pltpu.VMEM(labels_t.shape, f32),
            pltpu.VMEM((2, *centers.shape), f32),
            pltpu.VMEM((2, *weights_t.shape), f32),
            pltpu.VMEM((narrow, block, features), f32),
            pltpu.VMEM((narrow, block, owned), f32),
            pltpu.VMEM((narrow, block // 2, owned), f32),
            pltpu.VMEM((narrow, block // 2, outputs), f32),
            pltpu.VMEM((narrow, block, outputs), f32),
            pltpu.VMEM((last, outputs), f32),
            [pltpu.VMEM((narrow, held, outputs), f32) for held, _ in stages[1:]],
            pltpu.VMEM((narrow, last, outputs), f32),
            dma((4,)),
            dma((narrow,)), dma((narrow,)),
            dma((nst, narrow)), dma((nst, narrow)),
            dma((2,)), dma((2,)),
            dma((narrow,)), dma((narrow,)),
            dma((nst, narrow)), dma((nst, narrow)),
            dma((narrow,)), dma((narrow,)),
            dma((narrow,)), dma((narrow,)),
            dma((nst, narrow)), dma((nst, narrow)),
            dma((2,)),
        ],
        compiler_params=pltpu.CompilerParams(
            collective_id=0, has_side_effects=True, vmem_limit_bytes=60 * 2**20
        ),
    )(batch_index, train_features, labels_t, centers, weights_t)
    return new_weights_t.T, residual


def solution(mesh):
    in_specs = (
        P("narrow"),
        P("narrow", None),
        P("narrow", None),
        P(("wide", "narrow"), None),
        P(("wide", "narrow"), None),
    )
    out_specs = (P(("wide", "narrow"), None), P("narrow", None))
    return jax.shard_map(
        per_device, mesh=mesh, in_specs=in_specs, out_specs=out_specs, check_vma=False
    )
```

time: 57.2 us -> 55.8 us (0.976)
  the two profiles are of different devices: /device:TPU:25 before, /device:TPU:0 now
where the time goes in v2:
time: 55.8 us; the launch traced here: 55.7 us
  Pallas kernels  52 us (93%)
  local copies, waits for them, and re-layouts  2.99 us (5%)
  between operations  0.65 us (1%)
    pallas_call x1, Pallas kernels, per_device(): pl.pallas_call(functools.partial(step_kernel, wide, narrow, owned * wide...  52 us
    unnamed x4, local copies, waits for them, and re-layouts  2.99 us

profile of v2, /device:TPU:0, one launch (start us, length us, event | category | flops | bytes accessed | tf_op | source)
XLA Modules:
  0.0 55.7 jit_solution(1671333725486078324)
XLA Ops:
  0.6 52.0 %shard_map.68 = (f32[1000,256]{1,0:T(8,128)}, f32[64,1000]{1,0:T(8,128)}) custom-call(s32[64]{0:T(128)} %index_ref.1, f32[256,1024]{1,0:T(8,128)} %tf_hbm.1, f32[1000,256]{1,0:T(8,128)} %bitcast.3, f32[256,1024]{1,0:T(8,128)} %cen_hbm.1, f32[1000,256]{1,0:T(8,128)} %bitcast.4), custom_call_target="tpu_custom_call" | custom-call | tf_op jit(solution)/shard_map/pallas_call | solution.py:239
  52.7 0.0 copy-start
  52.7 2.3 %copy.9 = f32[256,1000]{0,1:T(8,128)} copy(f32[256,1000]{0,1:T(8,128)} %bitcast.5) | data formatting | bytes 2048000
  55.0 0.0 copy-done
  55.0 0.7 %copy.10 = f32[64,1000]{1,0:T(8,128)} copy(f32[64,1000]{1,0:T(8,128)S(1)} %copy-done) | data formatting | bytes 512000
Async XLA Ops:
  52.7 2.3 %copy-start = (f32[64,1000]{1,0:T(8,128)S(1)}, f32[64,1000]{1,0:T(8,128)}, u32[]{:S(2)}) copy-start(f32[64,1000]{1,0:T(8,128)} %get-tuple-element.9) | copy-start | bytes 768004

commit v3 on v2

--- a/solution.py
+++ b/solution.py
@@ -11,7 +11,7 @@
 step_size = 1.0
 MESH = pl.DeviceIdType.MESH
 HIGHEST = lax.Precision.HIGHEST
-ROW_DEPTH = 3
+ROW_DEPTH = 2
 SUB = 8
 
 
@@ -19,6 +19,31 @@
     return lax.dot_general(
         a, b, (dims, ((), ())), precision=HIGHEST, preferred_element_type=jnp.float32
     )
+
+
+def split(x, count):
+    terms = []
+    for _ in range(count):
+        terms.append(x.astype(jnp.bfloat16))
+        x = x - terms[-1].astype(jnp.float32)
+    return terms
+
+
+def split_dot(a, b):
+    held = a[0].shape[0]
+    orders = [[] for _ in a]
+    for i, right in enumerate(b):
+        left = a[: len(a) - i]
+        out = lax.dot_general(
+            jnp.concatenate(left, axis=0), right, (((1,), (1,)), ((), ())),
+            preferred_element_type=jnp.float32,
+        )
+        for j in range(len(left)):
+            orders[i + j].append(out[j * held : (j + 1) * held])
+    total = 0.0
+    for terms in orders[::-1]:
+        total = total + sum(terms)
+    return total
 
 
 def plan(wide, block):
@@ -31,8 +56,8 @@
 
 
 def step_kernel(
-    wide, narrow, count, index_ref, tf_hbm, lab_hbm, cen_hbm, wgt_hbm, out_hbm, res_hbm,
-    tf, lab, cen, wgt, rows, kern, away, part, resid, tgt, got, zgot, load_sem,
+    wide, narrow, count, index_ref, tf_hbm, lab_hbm, cen_hbm, wgt_hbm, kern_hbm, all_hbm, res_hbm,
+    tf, lab, cen, wgt, cen_terms, wgt_terms, rows, kern, away, part, resid, tgt, got, zgot, load_sem,
     zrow_s, zrow_r, row_s, row_r, pair_s, pair_r, kern_s, kern_r, red_s, red_r, zred_s, zred_r, zag_s, zag_r, ag_s, ag_r, out_sem,
 ):
     w, n = lax.axis_index("wide"), lax.axis_index("narrow")
@@ -125,6 +150,8 @@
 
     def squares(o):
         centers = cen[o]
+        for i, term in enumerate(split(centers, 3)):
+            cen_terms[o, i] = term
         return dot(ones, centers * centers, ((1,), (1,)))[0:1, :]
 
     center_sq = [squares(0)]
@@ -143,12 +170,13 @@
     def begin(ks):
         piece = jnp.concatenate([rows[at(k), mine, :] for k in ks], axis=0)
         piece_sq = jnp.sum(piece * piece, axis=1, keepdims=True)
+        piece_terms = split(piece, 3)
         total = 0.0
         for o in range(2):
             if len(center_sq) == o:
                 copy(cen.at[0], cen.at[1], pair_s.at[0], pair_r.at[0], partner).wait_recv()
                 center_sq.append(squares(o))
-            inner = dot(piece, cen[o], ((1,), (1,)))
+            inner = split_dot(piece_terms, [cen_terms[o, i] for i in range(3)])
             value = jnp.exp((2.0 * features - piece_sq - center_sq[o] + 2.0 * inner) / 128.0)
             for i, k in enumerate(ks):
                 this = value[i * half : (i + 1) * half, :]
@@ -158,7 +186,10 @@
                     away[k] = this
             if o == 1 and 0 in ks:
                 copy(wgt.at[0], wgt.at[1], pair_s.at[1], pair_r.at[1], partner).wait_recv()
-            total = total + dot(value, wgt[o], ((1,), (1,)))
+            if 0 in ks:
+                for i, term in enumerate(split(wgt[o], 2)):
+                    wgt_terms[o, i] = term
+            total = total + split_dot(split(value, 2), [wgt_terms[o, i] for i in range(2)])
         for i, k in enumerate(ks):
             part[at(k)] = total[i * half : (i + 1) * half, :]
         for k in ks:
@@ -206,25 +237,25 @@
     resid[n, keep, :] = total * (1.0 / math.sqrt(count)) - tgt[...]
 
     along_narrow(resid, keep, (zag_s, zag_r))
-    res_copy = pltpu.make_async_copy(resid.at[n], res_hbm, out_sem.at[0])
+    for k in range(narrow):
+        copy(away.at[k], kern.at[at(k), other], kern_s.at[k], kern_r.at[k], partner).wait_recv()
+    outs = [pltpu.make_async_copy(kern, kern_hbm, out_sem.at[0])]
+    outs[0].start()
     for t in range(narrow + len(cuts)):
         for i in range(len(cuts) + 1):
             if 0 <= t - i < narrow:
                 spread(resid, (zag_s, zag_r), (ag_s, ag_r), cuts, i, t - i)
-                if i == len(cuts) and t - i == 0:
-                    res_copy.start()
-
-    for k in range(narrow):
-        copy(away.at[k], kern.at[at(k), other], kern_s.at[k], kern_r.at[k], partner).wait_recv()
+                if i == len(cuts):
+                    m = at(t - i)
+                    outs.append(pltpu.make_async_copy(resid.at[m], all_hbm.at[m], out_sem.at[1 + t - i]))
+                    outs[-1].start()
+                    if t == i:
+                        outs.append(pltpu.make_async_copy(resid.at[n], res_hbm, out_sem.at[1 + narrow]))
+                        outs[-1].start()
     for c in sent:
         c.wait_send()
-    every = resid[...].reshape(batch, resid.shape[2])
-    delta = dot(every, kern[...].reshape(batch, owned), ((0,), (0,)))
-    wgt[0] = wgt[0] - step_size / batch * delta
-    out_copy = pltpu.make_async_copy(wgt.at[0], out_hbm, out_sem.at[1])
-    out_copy.start()
-    res_copy.wait()
-    out_copy.wait()
+    for c in outs:
+        c.wait()
 
 
 def per_device(batch_index, train_features, train_labels, centers, weights):
@@ -236,19 +267,22 @@
     nst, last = len(stages), stages[-1][0]
     f32, dma = jnp.float32, pltpu.SemaphoreType.DMA
     anywhere = pl.BlockSpec(memory_space=pl.ANY)
-    new_weights_t, residual = pl.pallas_call(
+    kernel, every, residual = pl.pallas_call(
         functools.partial(step_kernel, wide, narrow, owned * wide * narrow),
         out_shape=(
-            jax.ShapeDtypeStruct(weights_t.shape, f32),
+            jax.ShapeDtypeStruct((narrow, block, owned), f32),
+            jax.ShapeDtypeStruct((narrow, block, outputs), f32),
             jax.ShapeDtypeStruct((block, outputs), f32),
         ),
         in_specs=[pl.BlockSpec(memory_space=pltpu.SMEM)] + [anywhere] * 4,
-        out_specs=(anywhere, anywhere),
+        out_specs=(anywhere, anywhere, anywhere),
         scratch_shapes=[
             pltpu.VMEM(train_features.shape, f32),
             pltpu.VMEM(labels_t.shape, f32),
             pltpu.VMEM((2, *centers.shape), f32),
             pltpu.VMEM((2, *weights_t.shape), f32),
+            pltpu.VMEM((2, 3, *centers.shape), jnp.bfloat16),
+            pltpu.VMEM((2, 2, *weights_t.shape), jnp.bfloat16),
             pltpu.VMEM((narrow, block, features), f32),
             pltpu.VMEM((narrow, block, owned), f32),
             pltpu.VMEM((narrow, block // 2, owned), f32),
@@ -266,13 +300,18 @@
             dma((narrow,)), dma((narrow,)),
             dma((narrow,)), dma((narrow,)),
             dma((nst, narrow)), dma((nst, narrow)),
-            dma((2,)),
+            dma((2 + narrow,)),
         ],
         compiler_params=pltpu.CompilerParams(
             collective_id=0, has_side_effects=True, vmem_limit_bytes=60 * 2**20
         ),
     )(batch_index, train_features, labels_t, centers, weights_t)
-    return new_weights_t.T, residual
+    batch = narrow * block
+    delta = lax.dot_general(
+        kernel.reshape(batch, owned), every.reshape(batch, outputs), (((0,), (0,)), ((), ())),
+        precision=lax.Precision.HIGH, preferred_element_type=f32,
+    )
+    return weights - step_size / batch * delta, residual
 
 
 def solution(mesh):

time: 55.8 us -> 51 us (0.914); the launches traced: 55.7 us -> 50.3 us
  Pallas kernels: 52 us -> 45.6 us
  matrix products: 0 us -> 3.31 us
  local copies, waits for them, and re-layouts: 2.99 us -> 0.71 us
    pallas_call x1, Pallas kernels: 52 us -> 45.6 us  [per_device(): pl.pallas_call(functools.partial(step_kernel, wide, narrow, owned * wide...]
    dot_general x0 -> x1, matrix products: none -> 3.31 us  [per_device(): lax.dot_general(kernel.reshape(batch, owned), every.reshape(batch, output...]
    unnamed x4 -> x5, local copies, waits for them, and re-layouts: 2.99 us -> 0.71 us
where the time goes in v3:
time: 51 us; the launch traced here: 50.3 us
  Pallas kernels  45.6 us (89%)
  matrix products  3.31 us (6%)
  local copies, waits for them, and re-layouts  0.71 us (1%)
  between operations  0.66 us (1%)
    pallas_call x1, Pallas kernels, per_device(): pl.pallas_call(functools.partial(step_kernel, wide, narrow, owned * wide...  45.6 us
    dot_general x1, matrix products, per_device(): lax.dot_general(kernel.reshape(batch, owned), every.reshape(batch, output...  3.31 us

profile of v3, /device:TPU:0, one launch (start us, length us, event | category | flops | bytes accessed | tf_op | source)
XLA Modules:
  0.0 50.3 jit_solution(9850796575054628755)
XLA Ops:
  0.6 0.0 copy-start
  0.6 45.6 %shard_map.68 = (f32[4,64,256]{2,1,0:T(8,128)}, f32[4,64,1000]{2,1,0:T(8,128)}, f32[64,1000]{1,0:T(8,128)}) custom-call(s32[64]{0:T(128)} %index_ref.1, f32[256,1024]{1,0:T(8,128)} %tf_hbm.1, f32[1000,256]{1,0:T(8,128)} %bitcast.11, f32[256,1024]{1,0:T(8,128)} %cen_hbm.1, f32[1000,256]{1,0:T(8,128)} %bitcast.10), custom_call_target="tpu_custom_call" | custom-call | tf_op jit(solution)/shard_map/pallas_call | solution.py:270
  46.2 0.0 copy-done
  46.2 0.0 copy-start.1
  46.2 3.3 %fusion.1 = f32[256,1000]{0,1:T(8,128)} fusion(f32[256,1000]{0,1:T(8,128)S(1)} %copy-done, f32[4,64,256]{2,1,0:T(8,128)} %get-tuple-element.5, f32[4,64,1000]{2,1,0:T(8,128)} %get-tuple-element.6), kind=kOutput, calls=%fused_computation.2 | convolution fusion | flops 393728000 | bytes 3334144 | tf_op jit(solution)/shard_map/dot_general | solution.py:310
  49.6 0.0 copy-done.1
  49.6 0.7 %copy.8 = f32[64,1000]{1,0:T(8,128)} copy(f32[64,1000]{1,0:T(8,128)S(1)} %copy-done.1) | data formatting | bytes 512000
Async XLA Ops:
  0.6 45.6 %copy-start = (f32[256,1000]{0,1:T(8,128)S(1)}, f32[256,1000]{0,1:T(8,128)}, u32[]{:S(2)}) copy-start(f32[256,1000]{0,1:T(8,128)} %param.9) | copy-start | bytes 3072004
  46.2 3.3 %copy-start.1 = (f32[64,1000]{1,0:T(8,128)S(1)}, f32[64,1000]{1,0:T(8,128)}, u32[]{:S(2)}) copy-start(f32[64,1000]{1,0:T(8,128)} %get-tuple-element.11) | copy-start | bytes 768004

commit v4 on v3

--- a/solution.py
+++ b/solution.py
@@ -241,17 +241,20 @@
         copy(away.at[k], kern.at[at(k), other], kern_s.at[k], kern_r.at[k], partner).wait_recv()
     outs = [pltpu.make_async_copy(kern, kern_hbm, out_sem.at[0])]
     outs[0].start()
-    for t in range(narrow + len(cuts)):
-        for i in range(len(cuts) + 1):
-            if 0 <= t - i < narrow:
-                spread(resid, (zag_s, zag_r), (ag_s, ag_r), cuts, i, t - i)
-                if i == len(cuts):
-                    m = at(t - i)
-                    outs.append(pltpu.make_async_copy(resid.at[m], all_hbm.at[m], out_sem.at[1 + t - i]))
-                    outs[-1].start()
-                    if t == i:
-                        outs.append(pltpu.make_async_copy(resid.at[n], res_hbm, out_sem.at[1 + narrow]))
-                        outs[-1].start()
+    tail = len(cuts)
+    order = [(0, 0), (1, 0)] if tail else [(0, 0)]
+    for i in range(tail + 1):
+        order += [(i, k) for k in range(1, narrow)]
+        order += [(i + 2, 0)] if i + 2 <= tail else []
+    for i, k in order:
+        spread(resid, (zag_s, zag_r), (ag_s, ag_r), cuts, i, k)
+        if i == tail:
+            m = at(k)
+            outs.append(pltpu.make_async_copy(resid.at[m], all_hbm.at[m], out_sem.at[1 + k]))
+            outs[-1].start()
+            if k == 0:
+                outs.append(pltpu.make_async_copy(resid.at[n], res_hbm, out_sem.at[1 + narrow]))
+                outs[-1].start()
     for c in sent:
         c.wait_send()
     for c in outs:

time: 51 us -> 50.6 us (level)
  no operation moved by 1% of the time
where the time goes in v4:
time: 50.6 us; the launch traced here: 49.9 us
  Pallas kernels  45.2 us (89%)
  matrix products  3.31 us (7%)
  local copies, waits for them, and re-layouts  0.71 us (1%)
  between operations  0.66 us (1%)
    pallas_call x1, Pallas kernels, per_device(): pl.pallas_call(functools.partial(step_kernel, wide, narrow, owned * wide...  45.2 us
    dot_general x1, matrix products, per_device(): lax.dot_general(kernel.reshape(batch, owned), every.reshape(batch, output...  3.31 us

profile of v4, /device:TPU:0, one launch (start us, length us, event | category | flops | bytes accessed | tf_op | source)
XLA Modules:
  0.0 49.9 jit_solution(6450379479462925770)
XLA Ops:
  0.6 0.0 copy-start
  0.6 45.2 %shard_map.68 = (f32[4,64,256]{2,1,0:T(8,128)}, f32[4,64,1000]{2,1,0:T(8,128)}, f32[64,1000]{1,0:T(8,128)}) custom-call(s32[64]{0:T(128)} %index_ref.1, f32[256,1024]{1,0:T(8,128)} %tf_hbm.1, f32[1000,256]{1,0:T(8,128)} %bitcast.11, f32[256,1024]{1,0:T(8,128)} %cen_hbm.1, f32[1000,256]{1,0:T(8,128)} %bitcast.10), custom_call_target="tpu_custom_call" | custom-call | tf_op jit(solution)/shard_map/pallas_call | solution.py:273
  45.8 0.0 copy-done
  45.8 0.0 copy-start.1
  45.9 3.3 %fusion.1 = f32[256,1000]{0,1:T(8,128)} fusion(f32[256,1000]{0,1:T(8,128)S(1)} %copy-done, f32[4,64,256]{2,1,0:T(8,128)} %get-tuple-element.5, f32[4,64,1000]{2,1,0:T(8,128)} %get-tuple-element.6), kind=kOutput, calls=%fused_computation.2 | convolution fusion | flops 393728000 | bytes 3334144 | tf_op jit(solution)/shard_map/dot_general | solution.py:313
  49.2 0.0 copy-done.1
  49.2 0.7 %copy.8 = f32[64,1000]{1,0:T(8,128)} copy(f32[64,1000]{1,0:T(8,128)S(1)} %copy-done.1) | data formatting | bytes 512000
Async XLA Ops:
  0.6 45.2 %copy-start = (f32[256,1000]{0,1:T(8,128)S(1)}, f32[256,1000]{0,1:T(8,128)}, u32[]{:S(2)}) copy-start(f32[256,1000]{0,1:T(8,128)} %param.9) | copy-start | bytes 3072004
  45.8 3.3 %copy-start.1 = (f32[64,1000]{1,0:T(8,128)S(1)}, f32[64,1000]{1,0:T(8,128)}, u32[]{:S(2)}) copy-start(f32[64,1000]{1,0:T(8,128)} %get-tuple-element.11) | copy-start | bytes 768004
